TPU v7x, 128 devices: a whole 4x4x4 slice. The times are simulated.
128 devices in a mesh: ka: 8 (over y, z_hi), sy: 4 (over x), sz: 4 (over z_lo, core).
Axes of the slice: x: 4, y: 4, z: 4 (z_hi: 2, z_lo: 2; z = z_hi * 2 + z_lo), core: 2. Of those that a mesh axis runs over, the one named last changes fastest.
Arguments:
- orbitals: bfloat16 [16, 4, 2, 32, 128, 128], P('ka', None, None, 'sy', 'sz'), may hold values from -7.5 to 7.5
- coefficients: float32 [16, 4], replicated, may hold values from -4 to 4
- local_pot: float32 [32, 128, 128], P('sy', 'sz'), may hold values from 0 to 2
- perturb: float32 [32, 128, 128], P('sy', 'sz'), may hold values from -4 to 6
- q_index: int32 [1], replicated, may hold values from 0 to 1023
Outputs:
- responses: bfloat16 [16, 4, 2, 32, 128, 128], P('ka', None, None, 'sy', 'sz')
- density: float32 [32, 128, 128], P('sy', 'sz', 'ka')
All inputs are finite; a program needn't handle non-finite values.
Results may differ from a plain program's by a relative error of at most 0.0035.
Values may be sent and summed in bfloat16 or wider, within the bound.
A program may use at most 64 MiB of HBM per device.

v0:
```python
import functools

import jax
import jax.numpy as jnp
from jax import lax
from jax.experimental import pallas as pl
from jax.experimental.pallas import tpu as pltpu
from jax.sharding import PartitionSpec as P

MESH = pl.DeviceIdType.MESH
F32 = jnp.float32
BF16 = jnp.bfloat16

UNIT = 0.2 * 0.5 / 12.0
EPSILON = 1e-6
BANDS = 4
GROUP = 4
PITCH = 40
LEAD = 8


def fold(value):
    return value[0:8] + value[8:16] + value[16:24] + value[24:32]


def kernel(
    sizes, q_ref, orb, coeffs, pot, pert, resp, dens,
    phi, mid_a, mid_b, stage, land_a, land_b, potv, pertv, w_one, w_two, ring, t0, t1, t2, accs, entries, cf, dacc,
    ysend, yrecv, zsend, zrecv, red_send, red_recv, dsend, drecv,
    load_sem, first_s, first_r, second_s, second_r, red_s, red_r, halo_s, halo_r, den_s, den_r,
):
    nka, nsy, nsz = sizes
    slots, fields, ny, nz, nx = phi.shape
    ka, sy, sz = lax.axis_index("ka"), lax.axis_index("sy"), lax.axis_index("sz")

    def ka_at(step):
        return {"ka": lax.rem(ka + step, nka)}

    def group_at(step):
        return {"sy": lax.rem(sy + step // nsz, nsy), "sz": lax.rem(sz + step % nsz, nsz)}

    members = nsy * nsz
    mids, lands = (mid_a, mid_b), (land_a, land_b)
    loads = [
        pltpu.make_async_copy(orb, phi, load_sem.at[0]),
        pltpu.make_async_copy(pert, pertv, load_sem.at[1]),
        pltpu.make_async_copy(pot, potv, load_sem.at[2]),
    ]
    for copy in loads:
        copy.start()

    barrier = pltpu.get_barrier_semaphore()
    peers = [ka_at(d) for d in range(1, nka)] + [group_at(d) for d in range(1, members)]
    for peer in peers:
        pl.semaphore_signal(barrier, inc=1, device_id=peer, device_id_type=MESH)
    pl.semaphore_wait(barrier, len(peers))

    def awaited(ref, sem):
        return pltpu.make_async_copy(ref, ref, sem)

    def routed(src, dst, send, recv):
        return [
            pltpu.make_async_remote_copy(
                src.at[d], dst.at[d], send, recv, device_id=ka_at(d), device_id_type=MESH
            )
            for d in range(1, nka)
        ]

    def piece(of):
        return jnp.bitwise_and(-q_ref[0] - of, nka - 1)

    for slot in range(slots):
        for copy in routed(orb.at[slot], mids[slot], first_s.at[slot], first_r.at[slot]):
            copy.start()

    for copy in loads:
        copy.wait()
    w_one[...] = 0.2 * potv[...] - 0.25
    w_two[...] = 0.4 * potv[...] - 0.5
    dacc[...] = jnp.zeros_like(dacc)

    row_at = lax.broadcasted_iota(jnp.int32, (nx, nx), 0)
    column_at = lax.broadcasted_iota(jnp.int32, (nx, nx), 1)
    apart = jnp.bitwise_and(row_at - column_at, nx - 1)
    circle = jnp.where(
        (apart == 1) | (apart == nx - 1), -16.0, jnp.where((apart == 2) | (apart == nx - 2), 1.0, 0.0)
    ).astype(BF16)
    ring[0:nx] = circle
    ring[nx : 2 * nx] = circle
    ones = jnp.ones((8, nx), BF16)
    entries[...] = jnp.zeros_like(entries)

    for slot in range(slots):
        mid, land = mids[slot], lands[slot]
        mid[0] = phi[slot, 0]
        awaited(mid.at[1:nka], first_r.at[slot]).wait()
        land[0] = mid[piece(0)]
        for d in range(1, nka):
            stage[slot, d] = mid[piece(d)]
        for copy in routed(stage.at[slot], land, second_s.at[slot], second_r.at[slot]):
            copy.start()

    def inner(slot):
        accs[...] = jnp.zeros_like(accs)

        def plane(y, carry):
            pe = pertv[y]
            source = [
                (pe * phi[slot, 2 * c, y].astype(F32), pe * phi[slot, 2 * c + 1, y].astype(F32))
                for c in range(BANDS)
            ]
            for b in range(BANDS):
                p_re = lands[slot][piece(2 * b), y].astype(F32)
                p_im = lands[slot][piece(2 * b + 1), y].astype(F32)
                at = 8 * (32 + b)
                accs[at : at + 8] += fold(p_re * p_re + p_im * p_im)
                for c in range(BANDS):
                    s_re, s_im = source[c]
                    at = 8 * (b * BANDS + c)
                    accs[at : at + 8] += fold(p_re * s_re + p_im * s_im)
                    at += 8 * 16
                    accs[at : at + 8] += fold(p_re * s_im - p_im * s_re)
            return carry

        awaited(lands[slot].at[1:nka], second_r.at[slot]).wait()
        lax.fori_loop(0, ny, plane, 0)

    def reduce_start(slot):
        count = 32 + BANDS
        summed = accs[pl.ds(0, count, stride=8)]
        for i in range(1, 8):
            summed = summed + accs[pl.ds(i, count, stride=8)]
        entries[0:32] = summed[0:32]
        for b in range(BANDS):
            norm = jnp.broadcast_to(summed[32 + b : 33 + b], (BANDS, nx))
            entries[64 + b * BANDS : 64 + (b + 1) * BANDS] = norm
            entries[80 + b * BANDS : 80 + (b + 1) * BANDS] = norm
        whole = entries[...]
        row = jnp.zeros((8, nx), F32)
        for _ in range(3):
            rounded = whole.astype(BF16)
            row = row + lax.dot_general(
                ones, rounded, (((1,), (1,)), ((), ())), preferred_element_type=F32
            )
            whole = whole - rounded.astype(F32)
        for d in range(members):
            red_send[slot, d] = row
        for d in range(1, members):
            pltpu.make_async_remote_copy(
                red_send.at[slot, d], red_recv.at[slot, d], red_s.at[slot], red_r.at[slot],
                device_id=group_at(d), device_id_type=MESH,
            ).start()

    def reduce_finish(slot):
        awaited(red_recv.at[slot, 1:members], red_r.at[slot]).wait()
        total = red_send[slot, 0]
        for d in range(1, members):
            total = total + red_recv[slot, d]
        coef = total / (pltpu.roll(total, 64, 1) + EPSILON)
        for i in range(32):
            cf[i] = jnp.broadcast_to(coef[:, i : i + 1], (8, nx))

    def project(slot):
        def plane(y, carry):
            for half in range(nz // 16):
                at = pl.ds(16 * half, 16)

                def tiles(value):
                    return value.reshape(2, 8, nx)

                pe = tiles(pertv[y, at])
                partner = [tiles(lands[slot][piece(i), y, at].astype(F32)) for i in range(fields)]
                row = pl.ds(pl.multiple_of(LEAD + y * PITCH + 16 * half, 8), 16)
                for c in range(BANDS):
                    out_re = pe * tiles(phi[slot, 2 * c, y, at].astype(F32))
                    out_im = pe * tiles(phi[slot, 2 * c + 1, y, at].astype(F32))
                    for b in range(BANDS):
                        c_re = cf[b * BANDS + c]
                        c_im = cf[16 + b * BANDS + c]
                        p_re, p_im = partner[2 * b], partner[2 * b + 1]
                        out_re = out_re - (c_re * p_re - c_im * p_im)
                        out_im = out_im - (c_im * p_re + c_re * p_im)
                    t0[slot * fields + 2 * c, row] = out_re.reshape(16, nx)
                    t0[slot * fields + 2 * c + 1, row] = out_im.reshape(16, nx)
            return carry

        lax.fori_loop(0, ny, plane, 0)

    up_y = {"sy": lax.rem(sy + 1, nsy)}
    down_y = {"sy": lax.rem(sy + nsy - 1, nsy)}
    up_z = {"sz": lax.rem(sz + 1, nsz)}
    down_z = {"sz": lax.rem(sz + nsz - 1, nsz)}

    def halo_copies(e, g):
        at = pl.ds(g * GROUP, GROUP)
        sides = (
            (ysend, yrecv, 0, up_y, 0), (ysend, yrecv, 1, down_y, 0),
            (zsend, zrecv, 0, up_z, 1), (zsend, zrecv, 1, down_z, 1),
        )
        return [
            pltpu.make_async_remote_copy(
                out.at[e, side, at], into.at[e, side, at],
                halo_s.at[e, g, i], halo_r.at[e, g, i], device_id=peer, device_id_type=MESH,
            )
            for out, into, side, peer, i in sides
        ]

    def send(e, t, g):
        def field(f, carry):
            for i in range(2):
                first = LEAD + i * PITCH
                last = LEAD + (ny - 2 + i) * PITCH
                ysend[e, 0, f, i] = t[f, last : last + nz].astype(BF16)
                ysend[e, 1, f, i] = t[f, first : first + nz].astype(BF16)
            high = [t[f, pl.ds(LEAD + nz - 2 + i, ny, stride=PITCH)] for i in range(2)]
            low = [t[f, pl.ds(LEAD + i, ny, stride=PITCH)] for i in range(2)]
            zsend[e, 0, f] = jnp.concatenate(high, 0).astype(BF16)
            zsend[e, 1, f] = jnp.concatenate(low, 0).astype(BF16)
            return carry

        lax.fori_loop(g * GROUP, (g + 1) * GROUP, field, 0)
        for copy in halo_copies(e, g):
            copy.start()

    def applied(e, t, f, y, plane, along_x, w):
        first = LEAD + y * PITCH
        near = plane[y + 1] + plane[y - 1]
        far = plane[y + 2] + plane[y - 2]
        near = near + (t[f, first + 1 : first + 1 + nz] + t[f, first - 1 : first - 1 + nz])
        far = far + (t[f, first + 2 : first + 2 + nz] + t[f, first - 2 : first - 2 + nz])
        unit = UNIT if e == 0 else 2.0 * UNIT
        return w[y] * plane[y] + unit * ((far + along_x[y * nz : (y + 1) * nz]) - 16.0 * near)

    def step(e, g, slot):
        at = pl.ds(g * GROUP, GROUP)
        for i, ref in enumerate((yrecv, zrecv)):
            awaited(ref.at[e, :, at], halo_r.at[e, g, i]).wait()
        t = (t0, t1, t2)[e]
        if e == 2:
            row = jnp.bitwise_and(ka + q_ref[0], nka - 1) * slots + slot
            c0, c1, c2, c3 = (coeffs[j, row] for j in range(4))
            c13 = c1 - c3

        def field(f, carry):
            for side, start in ((0, LEAD - 2), (1, LEAD + nz)):
                rows_in = zrecv[e, side, f].astype(F32)
                t[f, pl.ds(start, ny, stride=PITCH)] = rows_in[0:ny]
                t[f, pl.ds(start + 1, ny, stride=PITCH)] = rows_in[ny : 2 * ny]
            plane = {}
            for y in range(ny):
                first = LEAD + y * PITCH
                plane[y] = t[f, first : first + nz]
            whole = jnp.concatenate([plane[y] for y in range(ny)], 0)
            high = whole.astype(BF16)
            low = (whole - high.astype(F32)).astype(BF16)
            along_x = jnp.dot(
                jnp.concatenate([high, low], 1), ring[...], preferred_element_type=F32
            )
            for i in range(2):
                plane[i - 2] = yrecv[e, 0, f, i].astype(F32)
                plane[ny + i] = yrecv[e, 1, f, i].astype(F32)
            for y in range(ny):
                at = slice(LEAD + y * PITCH, LEAD + y * PITCH + nz)
                if e == 0:
                    t1[f, at] = applied(e, t, f, y, plane, along_x, w_one)
                elif e == 1:
                    t2[f, at] = applied(e, t, f, y, plane, along_x, w_two) - t0[f, at]
                else:
                    doubled = applied(e, t, f, y, plane, along_x, w_two)
                    answer = (c0 * t0[f, at] + c13 * t1[f, at]) + (c2 * plane[y] + c3 * doubled)
                    rounded = answer.astype(BF16)
                    i = f - slot * fields
                    resp[slot, i, y] = rounded
                    dacc[y] += phi[slot, i, y].astype(F32) * rounded.astype(F32)
            return carry

        lax.fori_loop(g * GROUP, (g + 1) * GROUP, field, 0)

    def groups(slot):
        per_slot = fields // GROUP
        return range(slot * per_slot, (slot + 1) * per_slot)

    def begin(slot):
        inner(slot)
        reduce_start(slot)

    def start_expansion(slot):
        reduce_finish(slot)
        project(slot)
        for g in groups(slot):
            send(0, t0, g)

    def advance(slot, e):
        for g in groups(slot):
            step(e, g, slot)
            if e == 0:
                send(1, t1, g)
            elif e == 1:
                send(2, t2, g)

    begin(0)
    start_expansion(0)
    begin(1)
    advance(0, 0)
    start_expansion(1)
    advance(0, 1)
    advance(1, 0)
    advance(0, 2)
    advance(1, 1)
    advance(1, 2)

    lanes = nx // nka
    lane_at = lax.broadcasted_iota(jnp.int32, (nz, nx), 1)
    scale = 2.0 / (slots * nka)
    block_at = lax.shift_right_logical(lane_at, lanes.bit_length() - 1)
    blocks = [dacc[y] * scale for y in range(ny)]
    stride = nka // 2
    while stride:
        odd = jnp.bitwise_and(block_at, stride) != 0
        for i in range(nka):
            if not i & stride:
                one, two = blocks[i], blocks[i + stride]
                blocks[i] = jnp.where(odd, pltpu.roll(two, stride * lanes, 1), one)
                blocks[i + stride] = jnp.where(odd, two, pltpu.roll(one, nx - stride * lanes, 1))
        stride //= 2
    for d in range(nka):
        dsend[d] = blocks[d]
    den_copies = [
        pltpu.make_async_remote_copy(
            dsend.at[lax.rem(ka + d, nka)], drecv.at[d], den_s, den_r,
            device_id=ka_at(d), device_id_type=MESH,
        )
        for d in range(1, nka)
    ]
    for copy in den_copies:
        copy.start()
    awaited(drecv.at[1:nka], den_r).wait()
    total = dsend[ka]
    for d in range(1, nka):
        total = total + drecv[d]
    dens[...] = jnp.transpose(total)

    awaited(dsend.at[1:nka], den_s).wait()
    for slot in range(slots):
        awaited(orb.at[slot, 1:nka], first_s.at[slot]).wait()
        awaited(stage.at[slot, 1:nka], second_s.at[slot]).wait()
        awaited(red_send.at[slot, 1:members], red_s.at[slot]).wait()
    for e in range(3):
        for g in range(slots * fields // GROUP):
            at = pl.ds(g * GROUP, GROUP)
            awaited(ysend.at[e, :, at], halo_s.at[e, g, 0]).wait()
            awaited(zsend.at[e, :, at], halo_s.at[e, g, 1]).wait()


def call(sizes, q_index, orb, coeffs, pot, pert):
    nka, nsy, nsz = sizes
    slots, fields, ny, nz, nx = orb.shape
    count = slots * fields
    groups = count // GROUP
    hbm = pl.BlockSpec(memory_space=pltpu.HBM)
    smem = pl.BlockSpec(memory_space=pltpu.SMEM)
    vmem = pl.BlockSpec(memory_space=pltpu.VMEM)
    dma = pltpu.SemaphoreType.DMA
    t_shape = (count, LEAD + ny * PITCH, nx)
    scratch = [
        pltpu.VMEM(orb.shape, BF16),
        pltpu.VMEM(orb.shape[1:], BF16),
        pltpu.VMEM(orb.shape[1:], BF16),
        pltpu.VMEM(orb.shape, BF16),
        pltpu.VMEM(orb.shape[1:], BF16),
        pltpu.VMEM(orb.shape[1:], BF16),
        pltpu.VMEM(pot.shape, F32),
        pltpu.VMEM(pot.shape, F32),
        pltpu.VMEM(pot.shape, F32),
        pltpu.VMEM(pot.shape, F32),
        pltpu.VMEM((2 * nx, nx), BF16),
        pltpu.VMEM(t_shape, F32),
        pltpu.VMEM(t_shape, F32),
        pltpu.VMEM(t_shape, F32),
        pltpu.VMEM((40 * 8, nx), F32),
        pltpu.VMEM((nx, nx), F32),
        pltpu.VMEM((32, 8, nx), F32),
        pltpu.VMEM(pot.shape, F32),
        pltpu.VMEM((3, 2, count, 2, nz, nx), BF16),
        pltpu.VMEM((3, 2, count, 2, nz, nx), BF16),
        pltpu.VMEM((3, 2, count, 2 * ny, nx), BF16),
        pltpu.VMEM((3, 2, count, 2 * ny, nx), BF16),
        pltpu.VMEM((slots, nsy * nsz, 8, nx), F32),
        pltpu.VMEM((slots, nsy * nsz, 8, nx), F32),
        pltpu.VMEM((nka, nz, nx), F32),
        pltpu.VMEM((nka, nz, nx), F32),
        dma((3,)),
        dma((slots,)),
        dma((slots,)),
        dma((slots,)),
        dma((slots,)),
        dma((slots,)),
        dma((slots,)),
        dma((3, groups, 2)),
        dma((3, groups, 2)),
        dma,
        dma,
    ]
    held = [pltpu.with_memory_space_constraint(x, pltpu.HBM) for x in (orb, pot, pert)]
    return pl.pallas_call(
        functools.partial(kernel, sizes),
        out_shape=(
            pltpu.VMEM(orb.shape, BF16),
            pltpu.VMEM((nx, nz), F32),
        ),
        in_specs=[smem, hbm, smem, hbm, hbm],
        out_specs=(vmem, vmem),
        scratch_shapes=scratch,
        compiler_params=pltpu.CompilerParams(
            collective_id=0, has_side_effects=True, vmem_limit_bytes=48 << 20
        ),
        name="respond",
    )(q_index, *held[:1], coeffs, *held[1:])


def body(sizes, orbitals, coefficients, local_pot, perturb, q_index):
    orb = orbitals.reshape((orbitals.shape[0], -1) + orbitals.shape[3:])
    responses, density = call(sizes, q_index, orb, coefficients.T, local_pot, perturb)
    ny, nz, nx = local_pot.shape
    density = density.reshape((ny, nx // sizes[0], nz)).transpose(0, 2, 1)
    return responses.reshape(orbitals.shape), density


def solution(mesh):
    sizes = (mesh.shape["ka"], mesh.shape["sy"], mesh.shape["sz"])
    return jax.shard_map(
        functools.partial(body, sizes),
        mesh=mesh,
        in_specs=(
            P("ka", None, None, "sy", "sz", None),
            P(),
            P("sy", "sz", None),
            P("sy", "sz", None),
            P(),
        ),
        out_specs=(P("ka", None, None, "sy", "sz", None), P("sy", "sz", "ka")),
        check_vma=False,
    )
```

profile of v0, /device:TPU:0, one launch (start us, length us, event | category | flops | bytes accessed | tf_op | source)
XLA Modules:
  0.0 70.9 jit_solution(6263530189080450295)
XLA Ops:
  1.3 0.0 copy-start
  1.3 0.7 copy-done
  2.0 67.4 %respond.1 = (bf16[2,8,8,32,128]{4,3,2,1,0:T(8,128)(2,1)S(1)}, f32[128,32]{1,0:T(8,128)S(1)}) custom-call(s32[1]{0:T(128)S(6)} %copy.11.q_ref, bf16[2,8,8,32,128]{4,3,2,1,0:T(8,128)(2,1)} %bitcast.9, f32[4,16]{1,0:T(4,128)S(1)} %bitcast.8, f32[8,32,128]{2,1,0:T(8,128)} %pot.1, f32[8,32,128]{2,1,0:T(8,128)} %pert.1), custom_call_target="tpu_custom_call" | custom-call | tf_op jit(solution)/shard_map/respond/pallas_call | solution.py:405
  69.3 1.0 %copy.9 = bf16[2,4,2,8,32,128]{5,4,3,2,1,0:T(8,128)(2,1)} copy(bf16[2,4,2,8,32,128]{5,4,3,2,1,0:T(8,128)(2,1)S(1)} %bitcast.6) | data formatting | bytes 2097152
  70.3 0.6 copy.10
Async XLA Ops:
  1.3 0.7 copy-start
where the time goes:
time: 71.1 us; the launch traced here: 70.9 us
  Pallas kernels  67.4 us (95%)
  local copies, waits for them, and re-layouts  2.28 us (3%)
  between operations  1.29 us (2%)
    pallas_call x1, Pallas kernels, call(): pl.pallas_call(functools.partial(kernel, sizes), out_shape=(pltpu.VMEM(or...  67.4 us
    unnamed x4, local copies, waits for them, and re-layouts  2.28 us

commit v1 on v0

--- a/solution.py
+++ b/solution.py
@@ -24,10 +24,11 @@
 
 
 def kernel(
-    sizes, q_ref, orb, coeffs, pot, pert, resp, dens,
-    phi, mid_a, mid_b, stage, land_a, land_b, potv, pertv, w_one, w_two, ring, t0, t1, t2, accs, entries, cf, dacc,
+    sizes, q_ref, orb, coeffs_in, pot, pert, resp, dens,
+    coeffs, phi, mid_a, mid_b, stage, land_a, land_b, potv, pertv, w_one, w_two, ring, t0, t1, t2, accs, entries, cf, dacc,
+    phi_y, phi_z, phi_zs, pert_y, pert_z, pert_zs, part_y_a, part_y_b, part_z_a, part_z_b, part_zs, zpack,
     ysend, yrecv, zsend, zrecv, red_send, red_recv, dsend, drecv,
-    load_sem, first_s, first_r, second_s, second_r, red_s, red_r, halo_s, halo_r, den_s, den_r,
+    load_sem, first_s, first_r, second_s, second_r, red_s, red_r, early_s, early_r, halo_s, halo_r, den_s, den_r,
 ):
     nka, nsy, nsz = sizes
     slots, fields, ny, nz, nx = phi.shape
@@ -41,10 +42,12 @@
 
     members = nsy * nsz
     mids, lands = (mid_a, mid_b), (land_a, land_b)
+    parts_y, parts_z = (part_y_a, part_y_b), (part_z_a, part_z_b)
     loads = [
         pltpu.make_async_copy(orb, phi, load_sem.at[0]),
         pltpu.make_async_copy(pert, pertv, load_sem.at[1]),
         pltpu.make_async_copy(pot, potv, load_sem.at[2]),
+        pltpu.make_async_copy(coeffs_in, coeffs, load_sem.at[3]),
     ]
     for copy in loads:
         copy.start()
@@ -54,6 +57,26 @@
     for peer in peers:
         pl.semaphore_signal(barrier, inc=1, device_id=peer, device_id_type=MESH)
     pl.semaphore_wait(barrier, len(peers))
+
+    up_y = {"sy": lax.rem(sy + 1, nsy)}
+    down_y = {"sy": lax.rem(sy + nsy - 1, nsy)}
+    up_z = {"sz": lax.rem(sz + 1, nsz)}
+    down_z = {"sz": lax.rem(sz + nsz - 1, nsz)}
+
+    def early(i, high, low, into, peers):
+        for src, side, peer in ((high, 0, peers[0]), (low, 1, peers[1])):
+            pltpu.make_async_remote_copy(
+                src, into.at[side], early_s.at[i], early_r.at[i], device_id=peer, device_id_type=MESH
+            ).start()
+
+    along_y, along_z = (up_y, down_y), (up_z, down_z)
+
+    def pack_z(read):
+        zpack[...] = read(slice(nz - 8, nz)).astype(F32).reshape(8 * ny, nx)
+        high = [zpack[pl.ds(6 + i, ny, stride=8)] for i in range(2)]
+        zpack[...] = read(slice(0, 8)).astype(F32).reshape(8 * ny, nx)
+        low = [zpack[pl.ds(i, ny, stride=8)] for i in range(2)]
+        return jnp.concatenate(high, 0), jnp.concatenate(low, 0)
 
     def awaited(ref, sem):
         return pltpu.make_async_copy(ref, ref, sem)
@@ -73,8 +96,23 @@
         for copy in routed(orb.at[slot], mids[slot], first_s.at[slot], first_r.at[slot]):
             copy.start()
 
+    for slot in range(slots):
+        early(slot, orb.at[slot, :, ny - 2 : ny], orb.at[slot, :, 0:2], phi_y.at[slot], along_y)
+    early(2, pert.at[ny - 2 : ny], pert.at[0:2], pert_y, along_y)
     for copy in loads:
         copy.wait()
+    for slot in range(slots):
+
+        def own_field(i, carry):
+            high, low = pack_z(lambda at: phi[slot, i, :, at])
+            phi_zs[0, slot, i] = high.astype(BF16)
+            phi_zs[1, slot, i] = low.astype(BF16)
+            return carry
+
+        lax.fori_loop(0, fields, own_field, 0)
+    pert_zs[0], pert_zs[1] = pack_z(lambda at: pertv[:, at])
+    early(3, phi_zs.at[0], phi_zs.at[1], phi_z, along_z)
+    early(4, pert_zs.at[0], pert_zs.at[1], pert_z, along_z)
     w_one[...] = 0.2 * potv[...] - 0.25
     w_two[...] = 0.4 * potv[...] - 0.5
     dacc[...] = jnp.zeros_like(dacc)
@@ -123,6 +161,8 @@
             return carry
 
         awaited(lands[slot].at[1:nka], second_r.at[slot]).wait()
+        land = lands[slot]
+        early(5 + slot, land.at[:, ny - 2 : ny], land.at[:, 0:2], parts_y[slot], along_y)
         lax.fori_loop(0, ny, plane, 0)
 
     def reduce_start(slot):
@@ -143,53 +183,98 @@
                 ones, rounded, (((1,), (1,)), ((), ())), preferred_element_type=F32
             )
             whole = whole - rounded.astype(F32)
-        for d in range(members):
-            red_send[slot, d] = row
+        red_send[slot] = row[0:1]
         for d in range(1, members):
             pltpu.make_async_remote_copy(
-                red_send.at[slot, d], red_recv.at[slot, d], red_s.at[slot], red_r.at[slot],
+                red_send.at[slot], red_recv.at[slot, d], red_s.at[slot], red_r.at[slot],
                 device_id=group_at(d), device_id_type=MESH,
             ).start()
 
     def reduce_finish(slot):
         awaited(red_recv.at[slot, 1:members], red_r.at[slot]).wait()
-        total = red_send[slot, 0]
+        total = red_send[slot]
         for d in range(1, members):
             total = total + red_recv[slot, d]
         coef = total / (pltpu.roll(total, 64, 1) + EPSILON)
         for i in range(32):
             cf[i] = jnp.broadcast_to(coef[:, i : i + 1], (8, nx))
 
+    def partner_z(slot):
+        def field(i, carry):
+            high, low = pack_z(lambda at: lands[slot][i, :, at])
+            part_zs[slot, 0, i] = high.astype(BF16)
+            part_zs[slot, 1, i] = low.astype(BF16)
+            return carry
+
+        lax.fori_loop(0, fields, field, 0)
+        early(7 + slot, part_zs.at[slot, 0], part_zs.at[slot, 1], parts_z[slot], along_z)
+
+    def projected(pe, own, partner):
+        def tiles(value):
+            return value.astype(F32).reshape(2, 8, nx)
+
+        pe = tiles(pe)
+        partner = [tiles(value) for value in partner]
+        out = []
+        for c in range(BANDS):
+            out_re = pe * tiles(own[2 * c])
+            out_im = pe * tiles(own[2 * c + 1])
+            for b in range(BANDS):
+                c_re = cf[b * BANDS + c]
+                c_im = cf[16 + b * BANDS + c]
+                p_re, p_im = partner[2 * b], partner[2 * b + 1]
+                out_re = out_re - (c_re * p_re - c_im * p_im)
+                out_im = out_im - (c_im * p_re + c_re * p_im)
+            out += [out_re.reshape(16, nx), out_im.reshape(16, nx)]
+        return out
+
     def project(slot):
+        every = range(fields)
+        land, part_y, part_z = lands[slot], parts_y[slot], parts_z[slot]
+        first_field = slot * fields
+
         def plane(y, carry):
             for half in range(nz // 16):
                 at = pl.ds(16 * half, 16)
-
-                def tiles(value):
-                    return value.reshape(2, 8, nx)
-
-                pe = tiles(pertv[y, at])
-                partner = [tiles(lands[slot][piece(i), y, at].astype(F32)) for i in range(fields)]
                 row = pl.ds(pl.multiple_of(LEAD + y * PITCH + 16 * half, 8), 16)
-                for c in range(BANDS):
-                    out_re = pe * tiles(phi[slot, 2 * c, y, at].astype(F32))
-                    out_im = pe * tiles(phi[slot, 2 * c + 1, y, at].astype(F32))
-                    for b in range(BANDS):
-                        c_re = cf[b * BANDS + c]
-                        c_im = cf[16 + b * BANDS + c]
-                        p_re, p_im = partner[2 * b], partner[2 * b + 1]
-                        out_re = out_re - (c_re * p_re - c_im * p_im)
-                        out_im = out_im - (c_im * p_re + c_re * p_im)
-                    t0[slot * fields + 2 * c, row] = out_re.reshape(16, nx)
-                    t0[slot * fields + 2 * c + 1, row] = out_im.reshape(16, nx)
+                out = projected(
+                    pertv[y, at],
+                    [phi[slot, i, y, at] for i in every],
+                    [land[piece(i), y, at] for i in every],
+                )
+                for i in every:
+                    t0[first_field + i, row] = out[i]
             return carry
 
         lax.fori_loop(0, ny, plane, 0)
 
-    up_y = {"sy": lax.rem(sy + 1, nsy)}
-    down_y = {"sy": lax.rem(sy + nsy - 1, nsy)}
-    up_z = {"sz": lax.rem(sz + 1, nsz)}
-    down_z = {"sz": lax.rem(sz + nsz - 1, nsz)}
+        def outer_plane(i, carry):
+            side, layer = lax.shift_right_logical(i, 1), jnp.bitwise_and(i, 1)
+            for half in range(nz // 16):
+                at = pl.ds(16 * half, 16)
+                out = projected(
+                    pert_y[side, layer, at],
+                    [phi_y[slot, side, f, layer, at] for f in every],
+                    [part_y[side, piece(f), layer, at] for f in every],
+                )
+                for f in every:
+                    yrecv[0, side, first_field + f, layer, at] = out[f].astype(BF16)
+            return carry
+
+        def outer_rows(side, carry):
+            out = projected(
+                pert_z[side],
+                [phi_z[side, slot, f] for f in every],
+                [part_z[side, piece(f)] for f in every],
+            )
+            for f in every:
+                zrecv[0, side, first_field + f] = out[f].astype(BF16)
+            return carry
+
+        awaited(part_y, early_r.at[5 + slot]).wait()
+        awaited(part_z, early_r.at[7 + slot]).wait()
+        lax.fori_loop(0, 4, outer_plane, 0)
+        lax.fori_loop(0, 2, outer_rows, 0)
 
     def halo_copies(e, g):
         at = pl.ds(g * GROUP, GROUP)
@@ -200,7 +285,7 @@
         return [
             pltpu.make_async_remote_copy(
                 out.at[e, side, at], into.at[e, side, at],
-                halo_s.at[e, g, i], halo_r.at[e, g, i], device_id=peer, device_id_type=MESH,
+                halo_s.at[e - 1, g, i], halo_r.at[e - 1, g, i], device_id=peer, device_id_type=MESH,
             )
             for out, into, side, peer, i in sides
         ]
@@ -233,8 +318,9 @@
 
     def step(e, g, slot):
         at = pl.ds(g * GROUP, GROUP)
-        for i, ref in enumerate((yrecv, zrecv)):
-            awaited(ref.at[e, :, at], halo_r.at[e, g, i]).wait()
+        if e:
+            for i, ref in enumerate((yrecv, zrecv)):
+                awaited(ref.at[e, :, at], halo_r.at[e - 1, g, i]).wait()
         t = (t0, t1, t2)[e]
         if e == 2:
             row = jnp.bitwise_and(ka + q_ref[0], nka - 1) * slots + slot
@@ -280,16 +366,6 @@
         per_slot = fields // GROUP
         return range(slot * per_slot, (slot + 1) * per_slot)
 
-    def begin(slot):
-        inner(slot)
-        reduce_start(slot)
-
-    def start_expansion(slot):
-        reduce_finish(slot)
-        project(slot)
-        for g in groups(slot):
-            send(0, t0, g)
-
     def advance(slot, e):
         for g in groups(slot):
             step(e, g, slot)
@@ -298,16 +374,21 @@
             elif e == 1:
                 send(2, t2, g)
 
-    begin(0)
-    start_expansion(0)
-    begin(1)
-    advance(0, 0)
-    start_expansion(1)
-    advance(0, 1)
-    advance(1, 0)
-    advance(0, 2)
-    advance(1, 1)
-    advance(1, 2)
+    for slot in range(slots):
+        inner(slot)
+        reduce_start(slot)
+        partner_z(slot)
+    for slot in range(slots):
+        awaited(phi_y.at[slot], early_r.at[slot]).wait()
+    for ref, i in ((pert_y, 2), (phi_z, 3), (pert_z, 4)):
+        awaited(ref, early_r.at[i]).wait()
+    for slot in range(slots):
+        reduce_finish(slot)
+        project(slot)
+        advance(slot, 0)
+    for e in range(1, 3):
+        for slot in range(slots):
+            advance(slot, e)
 
     lanes = nx // nka
     lane_at = lax.broadcasted_iota(jnp.int32, (nz, nx), 1)
@@ -344,12 +425,17 @@
     for slot in range(slots):
         awaited(orb.at[slot, 1:nka], first_s.at[slot]).wait()
         awaited(stage.at[slot, 1:nka], second_s.at[slot]).wait()
-        awaited(red_send.at[slot, 1:members], red_s.at[slot]).wait()
-    for e in range(3):
+        awaited(red_recv.at[slot, 1:members], red_s.at[slot]).wait()
+        awaited(phi_y.at[slot], early_s.at[slot]).wait()
+        awaited(parts_y[slot], early_s.at[5 + slot]).wait()
+        awaited(parts_z[slot], early_s.at[7 + slot]).wait()
+    for ref, i in ((pert_y, 2), (phi_z, 3), (pert_z, 4)):
+        awaited(ref, early_s.at[i]).wait()
+    for e in range(1, 3):
         for g in range(slots * fields // GROUP):
             at = pl.ds(g * GROUP, GROUP)
-            awaited(ysend.at[e, :, at], halo_s.at[e, g, 0]).wait()
-            awaited(zsend.at[e, :, at], halo_s.at[e, g, 1]).wait()
+            awaited(ysend.at[e, :, at], halo_s.at[e - 1, g, 0]).wait()
+            awaited(zsend.at[e, :, at], halo_s.at[e - 1, g, 1]).wait()
 
 
 def call(sizes, q_index, orb, coeffs, pot, pert):
@@ -358,11 +444,11 @@
     count = slots * fields
     groups = count // GROUP
     hbm = pl.BlockSpec(memory_space=pltpu.HBM)
-    smem = pl.BlockSpec(memory_space=pltpu.SMEM)
     vmem = pl.BlockSpec(memory_space=pltpu.VMEM)
     dma = pltpu.SemaphoreType.DMA
     t_shape = (count, LEAD + ny * PITCH, nx)
     scratch = [
+        pltpu.SMEM(coeffs.shape, F32),
         pltpu.VMEM(orb.shape, BF16),
         pltpu.VMEM(orb.shape[1:], BF16),
         pltpu.VMEM(orb.shape[1:], BF16),
@@ -381,41 +467,55 @@
         pltpu.VMEM((nx, nx), F32),
         pltpu.VMEM((32, 8, nx), F32),
         pltpu.VMEM(pot.shape, F32),
+        pltpu.VMEM((slots, 2, fields, 2, nz, nx), BF16),
+        pltpu.VMEM((2, slots, fields, 2 * ny, nx), BF16),
+        pltpu.VMEM((2, slots, fields, 2 * ny, nx), BF16),
+        pltpu.VMEM((2, 2, nz, nx), F32),
+        pltpu.VMEM((2, 2 * ny, nx), F32),
+        pltpu.VMEM((2, 2 * ny, nx), F32),
+        pltpu.VMEM((2, fields, 2, nz, nx), BF16),
+        pltpu.VMEM((2, fields, 2, nz, nx), BF16),
+        pltpu.VMEM((2, fields, 2 * ny, nx), BF16),
+        pltpu.VMEM((2, fields, 2 * ny, nx), BF16),
+        pltpu.VMEM((slots, 2, fields, 2 * ny, nx), BF16),
+        pltpu.VMEM((8 * ny, nx), F32),
         pltpu.VMEM((3, 2, count, 2, nz, nx), BF16),
         pltpu.VMEM((3, 2, count, 2, nz, nx), BF16),
         pltpu.VMEM((3, 2, count, 2 * ny, nx), BF16),
         pltpu.VMEM((3, 2, count, 2 * ny, nx), BF16),
-        pltpu.VMEM((slots, nsy * nsz, 8, nx), F32),
-        pltpu.VMEM((slots, nsy * nsz, 8, nx), F32),
+        pltpu.VMEM((slots, 1, nx), F32),
+        pltpu.VMEM((slots, nsy * nsz, 1, nx), F32),
         pltpu.VMEM((nka, nz, nx), F32),
         pltpu.VMEM((nka, nz, nx), F32),
-        dma((3,)),
+        dma((4,)),
         dma((slots,)),
         dma((slots,)),
         dma((slots,)),
         dma((slots,)),
         dma((slots,)),
         dma((slots,)),
-        dma((3, groups, 2)),
-        dma((3, groups, 2)),
+        dma((9,)),
+        dma((9,)),
+        dma((2, groups, 2)),
+        dma((2, groups, 2)),
         dma,
         dma,
     ]
-    held = [pltpu.with_memory_space_constraint(x, pltpu.HBM) for x in (orb, pot, pert)]
+    held = [pltpu.with_memory_space_constraint(x, pltpu.HBM) for x in (orb, coeffs, pot, pert)]
     return pl.pallas_call(
         functools.partial(kernel, sizes),
         out_shape=(
             pltpu.VMEM(orb.shape, BF16),
             pltpu.VMEM((nx, nz), F32),
         ),
-        in_specs=[smem, hbm, smem, hbm, hbm],
+        in_specs=[pl.BlockSpec(memory_space=pltpu.SMEM)] + [hbm] * 4,
         out_specs=(vmem, vmem),
         scratch_shapes=scratch,
         compiler_params=pltpu.CompilerParams(
             collective_id=0, has_side_effects=True, vmem_limit_bytes=48 << 20
         ),
         name="respond",
-    )(q_index, *held[:1], coeffs, *held[1:])
+    )(q_index, *held)
 
 
 def body(sizes, orbitals, coefficients, local_pot, perturb, q_index):

time: 71.1 us -> 64.9 us (0.913)
  Pallas kernels: 67.4 us -> 61.9 us
    pallas_call x1, Pallas kernels: 67.4 us -> 61.9 us  [call(): pl.pallas_call(functools.partial(kernel, sizes), out_shape=(pltpu.VMEM(or...]
    unnamed x4 -> x2, local copies, waits for them, and re-layouts: 2.28 us -> 1.6 us
where the time goes in v1:
time: 64.9 us; the launch traced here: 64.7 us
  Pallas kernels  61.9 us (95%)
  local copies, waits for them, and re-layouts  1.6 us (2%)
  between operations  1.29 us (2%)
    pallas_call x1, Pallas kernels, call(): pl.pallas_call(functools.partial(kernel, sizes), out_shape=(pltpu.VMEM(or...  61.9 us
    unnamed x2, local copies, waits for them, and re-layouts  1.6 us

profile of v1, /device:TPU:0, one launch (start us, length us, event | category | flops | bytes accessed | tf_op | source)
XLA Modules:
  0.0 64.7 jit_solution(13430350313076426152)
XLA Ops:
  1.3 61.9 %respond.1 = (bf16[2,8,8,32,128]{4,3,2,1,0:T(8,128)(2,1)S(1)}, f32[128,32]{1,0:T(8,128)S(1)}) custom-call(s32[1]{0:T(128)S(6)} %copy.11.q_ref, bf16[2,8,8,32,128]{4,3,2,1,0:T(8,128)(2,1)} %bitcast.8, f32[4,16]{1,0:T(4,128)} %bitcast.9, f32[8,32,128]{2,1,0:T(8,128)} %pot.1, f32[8,32,128]{2,1,0:T(8,128)} %pert.1), custom_call_target="tpu_custom_call" | custom-call | tf_op jit(solution)/shard_map/respond/pallas_call | solution.py:505
  63.1 1.0 %copy.9 = bf16[2,4,2,8,32,128]{5,4,3,2,1,0:T(8,128)(2,1)} copy(bf16[2,4,2,8,32,128]{5,4,3,2,1,0:T(8,128)(2,1)S(1)} %bitcast.6) | data formatting | bytes 2097152
  64.1 0.6 copy.10

commit v2 on v1

--- a/solution.py
+++ b/solution.py
@@ -24,8 +24,8 @@
 
 
 def kernel(
-    sizes, q_ref, orb, coeffs_in, pot, pert, resp, dens,
-    coeffs, phi, mid_a, mid_b, stage, land_a, land_b, potv, pertv, w_one, w_two, ring, t0, t1, t2, accs, entries, cf, dacc,
+    sizes, q_in, orb, coeffs_in, pot, pert, resp, dens,
+    q_ref, coeffs, phi, mid_a, mid_b, stage, land_a, land_b, potv, pertv, w_one, w_two, ring, t0, t1, t2, accs, entries, cf, dacc,
     phi_y, phi_z, phi_zs, pert_y, pert_z, pert_zs, part_y_a, part_y_b, part_z_a, part_z_b, part_zs, zpack,
     ysend, yrecv, zsend, zrecv, red_send, red_recv, dsend, drecv,
     load_sem, first_s, first_r, second_s, second_r, red_s, red_r, early_s, early_r, halo_s, halo_r, den_s, den_r,
@@ -48,6 +48,7 @@
         pltpu.make_async_copy(pert, pertv, load_sem.at[1]),
         pltpu.make_async_copy(pot, potv, load_sem.at[2]),
         pltpu.make_async_copy(coeffs_in, coeffs, load_sem.at[3]),
+        pltpu.make_async_copy(q_in, q_ref, load_sem.at[4]),
     ]
     for copy in loads:
         copy.start()
@@ -161,8 +162,6 @@
             return carry
 
         awaited(lands[slot].at[1:nka], second_r.at[slot]).wait()
-        land = lands[slot]
-        early(5 + slot, land.at[:, ny - 2 : ny], land.at[:, 0:2], parts_y[slot], along_y)
         lax.fori_loop(0, ny, plane, 0)
 
     def reduce_start(slot):
@@ -199,7 +198,10 @@
         for i in range(32):
             cf[i] = jnp.broadcast_to(coef[:, i : i + 1], (8, nx))
 
-    def partner_z(slot):
+    def partner_halo(slot):
+        land = lands[slot]
+        early(5 + slot, land.at[:, ny - 2 : ny], land.at[:, 0:2], parts_y[slot], along_y)
+
         def field(i, carry):
             high, low = pack_z(lambda at: lands[slot][i, :, at])
             part_zs[slot, 0, i] = high.astype(BF16)
@@ -303,7 +305,7 @@
             zsend[e, 1, f] = jnp.concatenate(low, 0).astype(BF16)
             return carry
 
-        lax.fori_loop(g * GROUP, (g + 1) * GROUP, field, 0)
+        lax.fori_loop(g * GROUP, (g + 1) * GROUP, field, 0, unroll=2)
         for copy in halo_copies(e, g):
             copy.start()
 
@@ -360,7 +362,7 @@
                     dacc[y] += phi[slot, i, y].astype(F32) * rounded.astype(F32)
             return carry
 
-        lax.fori_loop(g * GROUP, (g + 1) * GROUP, field, 0)
+        lax.fori_loop(g * GROUP, (g + 1) * GROUP, field, 0, unroll=2)
 
     def groups(slot):
         per_slot = fields // GROUP
@@ -377,7 +379,7 @@
     for slot in range(slots):
         inner(slot)
         reduce_start(slot)
-        partner_z(slot)
+        partner_halo(slot)
     for slot in range(slots):
         awaited(phi_y.at[slot], early_r.at[slot]).wait()
     for ref, i in ((pert_y, 2), (phi_z, 3), (pert_z, 4)):
@@ -448,6 +450,7 @@
     dma = pltpu.SemaphoreType.DMA
     t_shape = (count, LEAD + ny * PITCH, nx)
     scratch = [
+        pltpu.SMEM(q_index.shape, jnp.int32),
         pltpu.SMEM(coeffs.shape, F32),
         pltpu.VMEM(orb.shape, BF16),
         pltpu.VMEM(orb.shape[1:], BF16),
@@ -487,7 +490,7 @@
         pltpu.VMEM((slots, nsy * nsz, 1, nx), F32),
         pltpu.VMEM((nka, nz, nx), F32),
         pltpu.VMEM((nka, nz, nx), F32),
-        dma((4,)),
+        dma((5,)),
         dma((slots,)),
         dma((slots,)),
         dma((slots,)),
@@ -508,7 +511,7 @@
             pltpu.VMEM(orb.shape, BF16),
             pltpu.VMEM((nx, nz), F32),
         ),
-        in_specs=[pl.BlockSpec(memory_space=pltpu.SMEM)] + [hbm] * 4,
+        in_specs=[pl.BlockSpec(memory_space=pl.ANY)] + [hbm] * 4,
         out_specs=(vmem, vmem),
         scratch_shapes=scratch,
         compiler_params=pltpu.CompilerParams(

time: 64.9 us -> 63.1 us (0.972)
  Pallas kernels: 61.9 us -> 60.1 us
    pallas_call x1, Pallas kernels: 61.9 us -> 60.1 us  [call(): pl.pallas_call(functools.partial(kernel, sizes), out_shape=(pltpu.VMEM(or...]
where the time goes in v2:
time: 63.1 us; the launch traced here: 63 us
  Pallas kernels  60.1 us (95%)
  local copies, waits for them, and re-layouts  1.6 us (3%)
  between operations  1.29 us (2%)
    pallas_call x1, Pallas kernels, call(): pl.pallas_call(functools.partial(kernel, sizes), out_shape=(pltpu.VMEM(or...  60.1 us
    unnamed x2, local copies, waits for them, and re-layouts  1.6 us

profile of v2, /device:TPU:0, one launch (start us, length us, event | category | flops | bytes accessed | tf_op | source)
XLA Modules:
  0.0 63.0 jit_solution(15771945250126447174)
XLA Ops:
  1.3 60.1 %respond.1 = (bf16[2,8,8,32,128]{4,3,2,1,0:T(8,128)(2,1)S(1)}, f32[128,32]{1,0:T(8,128)S(1)}) custom-call(s32[1]{0:T(128)S(6)} %copy.11.q_in, bf16[2,8,8,32,128]{4,3,2,1,0:T(8,128)(2,1)} %bitcast.8, f32[4,16]{1,0:T(4,128)} %bitcast.9, f32[8,32,128]{2,1,0:T(8,128)} %pot.1, f32[8,32,128]{2,1,0:T(8,128)} %pert.1), custom_call_target="tpu_custom_call" | custom-call | tf_op jit(solution)/shard_map/respond/pallas_call | solution.py:508
  61.4 1.0 %copy.9 = bf16[2,4,2,8,32,128]{5,4,3,2,1,0:T(8,128)(2,1)} copy(bf16[2,4,2,8,32,128]{5,4,3,2,1,0:T(8,128)(2,1)S(1)} %bitcast.6) | data formatting | bytes 2097152
  62.4 0.6 copy.10

commit v3 on v2

--- a/solution.py
+++ b/solution.py
@@ -24,11 +24,11 @@
 
 
 def kernel(
-    sizes, q_in, orb, coeffs_in, pot, pert, resp, dens,
+    shift, sizes, q_in, orb, coeffs_in, pot, pert, resp, dens,
     q_ref, coeffs, phi, mid_a, mid_b, stage, land_a, land_b, potv, pertv, w_one, w_two, ring, t0, t1, t2, accs, entries, cf, dacc,
     phi_y, phi_z, phi_zs, pert_y, pert_z, pert_zs, part_y_a, part_y_b, part_z_a, part_z_b, part_zs, zpack,
     ysend, yrecv, zsend, zrecv, red_send, red_recv, dsend, drecv,
-    load_sem, first_s, first_r, second_s, second_r, red_s, red_r, early_s, early_r, halo_s, halo_r, den_s, den_r,
+    load_sem, first_s, first_r, route_s, route_r, red_s, red_r, early_s, early_r, halo_s, halo_r, den_s, den_r,
 ):
     nka, nsy, nsz = sizes
     slots, fields, ny, nz, nx = phi.shape
@@ -42,6 +42,7 @@
 
     members = nsy * nsz
     mids, lands = (mid_a, mid_b), (land_a, land_b)
+    direct = shift is not None
     parts_y, parts_z = (part_y_a, part_y_b), (part_z_a, part_z_b)
     loads = [
         pltpu.make_async_copy(orb, phi, load_sem.at[0]),
@@ -82,20 +83,25 @@
     def awaited(ref, sem):
         return pltpu.make_async_copy(ref, ref, sem)
 
+    def piece(of):
+        return of if direct else jnp.bitwise_and(-q_ref[0] - of, nka - 1)
+
     def routed(src, dst, send, recv):
-        return [
+        for d in range(1, nka):
             pltpu.make_async_remote_copy(
                 src.at[d], dst.at[d], send, recv, device_id=ka_at(d), device_id_type=MESH
-            )
-            for d in range(1, nka)
-        ]
-
-    def piece(of):
-        return jnp.bitwise_and(-q_ref[0] - of, nka - 1)
+            ).start()
 
     for slot in range(slots):
-        for copy in routed(orb.at[slot], mids[slot], first_s.at[slot], first_r.at[slot]):
-            copy.start()
+        if not direct:
+            routed(orb.at[slot], mids[slot], first_s.at[slot], first_r.at[slot])
+        elif shift:
+            pltpu.make_async_remote_copy(
+                orb.at[slot], lands[slot], route_s.at[slot], route_r.at[slot],
+                device_id=ka_at(nka - shift), device_id_type=MESH,
+            ).start()
+        else:
+            pltpu.make_async_copy(orb.at[slot], lands[slot], route_r.at[slot]).start()
 
     for slot in range(slots):
         early(slot, orb.at[slot, :, ny - 2 : ny], orb.at[slot, :, 0:2], phi_y.at[slot], along_y)
@@ -129,15 +135,15 @@
     ones = jnp.ones((8, nx), BF16)
     entries[...] = jnp.zeros_like(entries)
 
-    for slot in range(slots):
-        mid, land = mids[slot], lands[slot]
-        mid[0] = phi[slot, 0]
-        awaited(mid.at[1:nka], first_r.at[slot]).wait()
-        land[0] = mid[piece(0)]
-        for d in range(1, nka):
-            stage[slot, d] = mid[piece(d)]
-        for copy in routed(stage.at[slot], land, second_s.at[slot], second_r.at[slot]):
-            copy.start()
+    if not direct:
+        for slot in range(slots):
+            mid, land = mids[slot], lands[slot]
+            mid[0] = phi[slot, 0]
+            awaited(mid.at[1:nka], first_r.at[slot]).wait()
+            land[0] = mid[piece(0)]
+            for d in range(1, nka):
+                stage[slot, d] = mid[piece(d)]
+            routed(stage.at[slot], land, route_s.at[slot], route_r.at[slot])
 
     def inner(slot):
         accs[...] = jnp.zeros_like(accs)
@@ -161,7 +167,8 @@
                     accs[at : at + 8] += fold(p_re * s_im - p_im * s_re)
             return carry
 
-        awaited(lands[slot].at[1:nka], second_r.at[slot]).wait()
+        landed = lands[slot] if direct else lands[slot].at[1:nka]
+        awaited(landed, route_r.at[slot]).wait()
         lax.fori_loop(0, ny, plane, 0)
 
     def reduce_start(slot):
@@ -278,6 +285,14 @@
         lax.fori_loop(0, 4, outer_plane, 0)
         lax.fori_loop(0, 2, outer_rows, 0)
 
+    def each(g, field):
+        def pair(i, carry):
+            for j in range(2):
+                field(g * GROUP + 2 * i + j, 0)
+            return carry
+
+        lax.fori_loop(0, GROUP // 2, pair, 0)
+
     def halo_copies(e, g):
         at = pl.ds(g * GROUP, GROUP)
         sides = (
@@ -305,7 +320,7 @@
             zsend[e, 1, f] = jnp.concatenate(low, 0).astype(BF16)
             return carry
 
-        lax.fori_loop(g * GROUP, (g + 1) * GROUP, field, 0, unroll=2)
+        each(g, field)
         for copy in halo_copies(e, g):
             copy.start()
 
@@ -325,7 +340,7 @@
                 awaited(ref.at[e, :, at], halo_r.at[e - 1, g, i]).wait()
         t = (t0, t1, t2)[e]
         if e == 2:
-            row = jnp.bitwise_and(ka + q_ref[0], nka - 1) * slots + slot
+            row = jnp.bitwise_and(ka + (shift if direct else q_ref[0]), nka - 1) * slots + slot
             c0, c1, c2, c3 = (coeffs[j, row] for j in range(4))
             c13 = c1 - c3
 
@@ -362,35 +377,51 @@
                     dacc[y] += phi[slot, i, y].astype(F32) * rounded.astype(F32)
             return carry
 
-        lax.fori_loop(g * GROUP, (g + 1) * GROUP, field, 0, unroll=2)
-
-    def groups(slot):
+        each(g, field)
+
+    def advance(slot, e):
         per_slot = fields // GROUP
-        return range(slot * per_slot, (slot + 1) * per_slot)
-
-    def advance(slot, e):
-        for g in groups(slot):
+
+        def group(g, carry):
             step(e, g, slot)
             if e == 0:
                 send(1, t1, g)
             elif e == 1:
                 send(2, t2, g)
-
-    for slot in range(slots):
+            return carry
+
+        lax.fori_loop(slot * per_slot, (slot + 1) * per_slot, group, 0)
+
+    def begin(slot):
         inner(slot)
         reduce_start(slot)
         partner_halo(slot)
+
+    def expand(slot):
+        reduce_finish(slot)
+        project(slot)
+        advance(slot, 0)
+
+    begin(0)
+    if not direct:
+        begin(1)
     for slot in range(slots):
         awaited(phi_y.at[slot], early_r.at[slot]).wait()
     for ref, i in ((pert_y, 2), (phi_z, 3), (pert_z, 4)):
         awaited(ref, early_r.at[i]).wait()
-    for slot in range(slots):
-        reduce_finish(slot)
-        project(slot)
-        advance(slot, 0)
-    for e in range(1, 3):
-        for slot in range(slots):
-            advance(slot, e)
+    expand(0)
+    if direct:
+        begin(1)
+        advance(0, 1)
+        expand(1)
+        advance(0, 2)
+        advance(1, 1)
+    else:
+        expand(1)
+        advance(0, 1)
+        advance(1, 1)
+        advance(0, 2)
+    advance(1, 2)
 
     lanes = nx // nka
     lane_at = lax.broadcasted_iota(jnp.int32, (nz, nx), 1)
@@ -425,8 +456,11 @@
 
     awaited(dsend.at[1:nka], den_s).wait()
     for slot in range(slots):
-        awaited(orb.at[slot, 1:nka], first_s.at[slot]).wait()
-        awaited(stage.at[slot, 1:nka], second_s.at[slot]).wait()
+        if not direct:
+            awaited(mids[slot].at[1:nka], first_s.at[slot]).wait()
+            awaited(lands[slot].at[1:nka], route_s.at[slot]).wait()
+        elif shift:
+            awaited(lands[slot], route_s.at[slot]).wait()
         awaited(red_recv.at[slot, 1:members], red_s.at[slot]).wait()
         awaited(phi_y.at[slot], early_s.at[slot]).wait()
         awaited(parts_y[slot], early_s.at[5 + slot]).wait()
@@ -440,7 +474,7 @@
             awaited(zsend.at[e, :, at], halo_s.at[e - 1, g, 1]).wait()
 
 
-def call(sizes, q_index, orb, coeffs, pot, pert):
+def call(shift, sizes, q_index, orb, coeffs, pot, pert):
     nka, nsy, nsz = sizes
     slots, fields, ny, nz, nx = orb.shape
     count = slots * fields
@@ -506,7 +540,7 @@
     ]
     held = [pltpu.with_memory_space_constraint(x, pltpu.HBM) for x in (orb, coeffs, pot, pert)]
     return pl.pallas_call(
-        functools.partial(kernel, sizes),
+        functools.partial(kernel, shift, sizes),
         out_shape=(
             pltpu.VMEM(orb.shape, BF16),
             pltpu.VMEM((nx, nz), F32),
@@ -515,15 +549,22 @@
         out_specs=(vmem, vmem),
         scratch_shapes=scratch,
         compiler_params=pltpu.CompilerParams(
-            collective_id=0, has_side_effects=True, vmem_limit_bytes=48 << 20
+            collective_id=1 if shift is None else shift, has_side_effects=True, vmem_limit_bytes=48 << 20
         ),
-        name="respond",
+        name=f"respond_{shift}",
     )(q_index, *held)
 
 
 def body(sizes, orbitals, coefficients, local_pot, perturb, q_index):
     orb = orbitals.reshape((orbitals.shape[0], -1) + orbitals.shape[3:])
-    responses, density = call(sizes, q_index, orb, coefficients.T, local_pot, perturb)
+    nka = sizes[0]
+    kinds = list(range(0, nka, 2)) + [None]
+    branches = [functools.partial(call, kind, sizes) for kind in kinds]
+    shift = q_index[0] % nka
+    chosen = jnp.where(shift % 2 == 0, shift // 2, len(kinds) - 1)
+    responses, density = lax.switch(
+        chosen, branches, q_index, orb, coefficients.T, local_pot, perturb
+    )
     ny, nz, nx = local_pot.shape
     density = density.reshape((ny, nx // sizes[0], nz)).transpose(0, 2, 1)
     return responses.reshape(orbitals.shape), density

time: 63.1 us -> 64.3 us (1.019)
  Pallas kernels: 60.1 us -> 60.8 us
    pallas_call x1, Pallas kernels: 60.1 us -> 60.8 us  [call(): pl.pallas_call(functools.partial(kernel, shift, sizes), out_shape=(pltpu....]
where the time goes in v3:
time: 64.3 us; the launch traced here: 64.2 us
  Pallas kernels  60.8 us (95%)
  local copies, waits for them, and re-layouts  1.6 us (2%)
  between operations  1.33 us (2%)
    pallas_call x1, Pallas kernels, call(): pl.pallas_call(functools.partial(kernel, shift, sizes), out_shape=(pltpu....  60.8 us
    unnamed x2, local copies, waits for them, and re-layouts  1.6 us

profile of v3, /device:TPU:0, one launch (start us, length us, event | category | flops | bytes accessed | tf_op | source)
XLA Modules:
  0.0 64.2 jit_solution(8034362989065722516)
XLA Ops:
  1.3 61.3 %conditional.1 = (f32[128,32]{1,0:T(8,128)S(1)}, bf16[2,4,2,8,32,128]{5,4,3,2,1,0:T(8,128)(2,1)S(1)}) conditional(s32[]{:T(128)} %clamp.3, (s32[1]{0:T(128)}, bf16[2,8,8,32,128]{4,3,2,1,0:T(8,128)(2,1)}, f32[4,16]{1,0:T(4,128)}, f32[8,32,128]{2,1,0:T(8,128)}, f32[8,32,128]{2,1,0:T(8,128)}) %tuple.47, (s32[1]{0:T(128)}, ...), branch_computations={%region_0.1_spmd, %region_1.2_spmd, %region_2.3_spmd, %region_3.4_... | conditional | bytes 16 | solution.py:565
  1.5 60.8 %respond_None.1 = (bf16[2,8,8,32,128]{4,3,2,1,0:T(8,128)(2,1)S(1)}, f32[128,32]{1,0:T(8,128)S(1)}) custom-call(s32[1]{0:T(128)} %get-tuple-element.89.q_in, bf16[2,8,8,32,128]{4,3,2,1,0:T(8,128)(2,1)} %get-tuple-element.90.orb, f32[4,16]{1,0:T(4,128)} %get-tuple-element.91.coeffs_in, f32[8,32,128]{2,1,0:T(8,128)} %get-tuple-element.92.pot, ...), custom_call_target="tpu_custom_call" | custom-call | tf_op jit(solution)/shard_map/cond/branch_4_fun/respond_None/pallas_call | solution.py:542
  62.6 1.0 %copy.19 = bf16[2,4,2,8,32,128]{5,4,3,2,1,0:T(8,128)(2,1)} copy(bf16[2,4,2,8,32,128]{5,4,3,2,1,0:T(8,128)(2,1)S(1)} %get-tuple-element.112) | data formatting | bytes 2097152
  63.6 0.6 copy.20
